TPU v7x, 256 devices: a whole 4x4x8 slice. The times are simulated.
256 devices in a mesh: dp: 32 (over y, z), tensor: 8 (over x, core).
Axes of the slice: x: 4, y: 4, z: 8, core: 2. Of those that a mesh axis runs over, the one named last changes fastest.
Arguments:
- queries: bfloat16 [256, 6, 8192], P('dp', None, 'tensor'), may hold values from -150 to 150
- new_keys: bfloat16 [256, 6, 1024], P('dp', None, 'tensor'), may hold values from -6 to 6
- new_values: bfloat16 [256, 6, 1024], P('dp', None, 'tensor'), may hold values from -6 to 6
- key_cache: bfloat16 [256, 256, 1024], P('dp', None, 'tensor'), may hold values from -6 to 6
- value_cache: bfloat16 [256, 256, 1024], P('dp', None, 'tensor'), may hold values from -6 to 6
- cache_lengths: int32 [256], P('dp'), may hold values from 32 to 256, as said below
- accepted: int32 [256], P('tensor'), may hold values from 1 to 6
- residual: bfloat16 [256, 6, 8192], P('tensor', None, 'dp'), may hold values from -6 to 6
- out_weight: bfloat16 [8192, 8192], P('tensor', 'dp'), may hold values from -0.0625 to 0.0625
- draft_weight: bfloat16 [8192, 8192], P('tensor', 'dp'), may hold values from -0.0625 to 0.0625
Outputs:
- verified: bfloat16 [256, 6, 8192], P('tensor', None, 'dp')
- drafted: bfloat16 [5, 256, 8192], P(None, 'tensor', 'dp')
Inputs may be any that keep to these rules, and one draw needn't show every extreme that they name: `cache_lengths`: every draw has a window with all 256 slots live.
All inputs are finite; a program needn't handle non-finite values.
Results may differ from a plain program's by a relative error of at most 0.008.
Values may be sent and summed in bfloat16 or wider, within the bound.
No kernel may reach another device: no remote copies, remote signals or barrier semaphores. Data moves between devices by JAX's collectives and lax.ppermute only.
A program may use at most 64 MiB of HBM per device.

v0:
```python
import jax
import jax.numpy as jnp
from jax import lax
from jax.sharding import PartitionSpec as P

HD = 128
STEPS = 5


def widen(drafted_rows):
    wide_rows = lax.all_gather(drafted_rows, "dp", axis=1, tiled=True)
    return lax.all_to_all(wide_rows, "tensor", split_axis=1, concat_axis=0, tiled=True)


def per_device(
    queries,
    new_keys,
    new_values,
    key_cache,
    value_cache,
    cache_lengths,
    accepted,
    residual,
    out_weight,
    draft_weight,
):
    windows_here, tokens_here, query_width = queries.shape
    cache_size = key_cache.shape[1]
    kv_here = new_keys.shape[2] // HD
    group_size = query_width // HD // kv_here
    query_split = queries.reshape(windows_here, tokens_here, kv_here, group_size, HD)
    keys_cached = key_cache.reshape(windows_here, cache_size, kv_here, HD)
    keys_fresh = new_keys.reshape(windows_here, tokens_here, kv_here, HD)
    score_cache = jnp.einsum(
        "wtkgd,wpkd->wkgtp", query_split, keys_cached, preferred_element_type=jnp.float32
    ) * HD ** (-0.5)
    score_fresh = jnp.einsum(
        "wtkgd,wpkd->wkgtp", query_split, keys_fresh, preferred_element_type=jnp.float32
    ) * HD ** (-0.5)
    live_cache = (jnp.arange(cache_size)[None, :] < cache_lengths[:, None])[:, None, None, None, :]
    live_fresh = jnp.arange(tokens_here)[None, :] <= jnp.arange(tokens_here)[:, None]
    scores = jnp.concatenate(
        [
            jnp.where(live_cache, score_cache, -jnp.inf),
            jnp.where(live_fresh, score_fresh, -jnp.inf),
        ],
        axis=-1,
    )
    largest = jnp.max(scores, axis=-1, keepdims=True)
    powered = jnp.exp(scores - largest)
    weights = (powered / jnp.sum(powered, axis=-1, keepdims=True)).astype(jnp.bfloat16)
    values_cached = value_cache.reshape(windows_here, cache_size, kv_here, HD)
    values_fresh = new_values.reshape(windows_here, tokens_here, kv_here, HD)
    mixed_rows = jnp.einsum(
        "wkgtp,wpkd->wtkgd",
        weights[..., :cache_size],
        values_cached,
        preferred_element_type=jnp.float32,
    )
    mixed_rows = mixed_rows + jnp.einsum(
        "wkgtp,wpkd->wtkgd",
        weights[..., cache_size:],
        values_fresh,
        preferred_element_type=jnp.float32,
    )
    attended = mixed_rows.astype(jnp.bfloat16).reshape(windows_here * tokens_here, query_width)
    partial_out = jnp.dot(
        lax.all_gather(attended, "dp", axis=0, tiled=True),
        out_weight,
        preferred_element_type=jnp.float32,
    )
    summed = lax.psum_scatter(partial_out, "tensor", scatter_dimension=0, tiled=True)
    block_windows, block_tokens, block_cols = residual.shape
    flat_residual = residual.reshape(block_windows * block_tokens, block_cols).astype(jnp.float32)
    verified = (
        (flat_residual + summed)
        .astype(jnp.bfloat16)
        .reshape(block_windows, block_tokens, block_cols)
    )
    chosen = jnp.arange(block_tokens)[None, :] == (accepted - 1)[:, None]
    picked = jnp.sum(
        jnp.where(chosen[:, :, None], verified, jnp.zeros((), jnp.bfloat16)),
        axis=1,
        dtype=jnp.bfloat16,
    )
    results = []
    current = widen(picked)
    row_block = current.shape[0] // lax.axis_size("tensor")
    row_start = lax.axis_index("tensor") * row_block
    for draft_step in range(STEPS):
        everyone = lax.psum(
            jnp.dot(current, draft_weight, preferred_element_type=jnp.float32), "tensor"
        )
        share = lax.dynamic_slice_in_dim(everyone, row_start, row_block, 0)
        drafted_now = jnp.tanh(2.0 * share).astype(jnp.bfloat16)
        results.append(drafted_now)
        if draft_step + 1 < STEPS:
            current = widen(drafted_now)
    return (verified, jnp.stack(results))


def solution(mesh):
    placed = (
        P("dp", None, "tensor"),
        P("dp", None, "tensor"),
        P("dp", None, "tensor"),
        P("dp", None, "tensor"),
        P("dp", None, "tensor"),
        P("dp"),
        P("tensor"),
        P("tensor", None, "dp"),
        P("tensor", "dp"),
        P("tensor", "dp"),
    )
    return jax.shard_map(
        per_device,
        mesh=mesh,
        in_specs=placed,
        out_specs=(P("tensor", None, "dp"), P(None, "tensor", "dp")),
        check_vma=False,
    )
```

profile of v0, /device:TPU:8, one launch (start us, length us, event | category | flops | bytes accessed | tf_op | source)
XLA Modules:
  0.0 744.6 jit_solution(10365520250779408295)
XLA Ops:
  7.2 0.8 iota_compare_fusion.1
  8.1 1.4 fusion.17
  9.5 1.2 fusion.18
  11.1 0.9 fusion.10
  13.0 81.7 %all-gather.2.cloned.1.call-done = bf16[1536,1024]{1,0:T(8,128)(2,1)} async-done(((bf16[48,1024]{1,0:T(8,128)(2,1)}), bf16[1536,1024]{1,0:T(8,128)(2,1)}) %all-gather.2.cloned.1.call-update) | async-done | bytes 3145744 | tf_op jit(solution)/shard_map/all_gather | solution.py:68
  94.7 4.0 fusion.19
  99.0 32.9 %reduce-scatter.2.cloned.1.call-done = f32[192,256]{1,0:T(8,128)} async-done(((f32[1536,256]{1,0:T(8,128)}), f32[192,256]{1,0:T(8,128)}) %reduce-scatter.2.cloned.1.call-update) | async-done | bytes 196624 | tf_op jit(solution)/shard_map/reduce_scatter | solution.py:72
  131.9 0.9 add_convert_fusion
  133.0 43.9 %all_gather.19 = bf16[32,8192]{1,0:T(8,128)(2,1)S(1)} all-gather(bf16[32,256]{1,0:T(8,128)(2,1)S(1)} %select_reduce_fusion), channel_id=1, replica_groups=mesh['dp'=32,'tensor'=8] {'dp'}, dimensions={1}, use_global_device_ids=true | all-gather | bytes 540672 | tf_op jit(solution)/shard_map/all_gather | solution.py:11
  177.0 12.8 %all_to_all.95 = bf16[32,8,1024]{2,0,1:T(8,128)(2,1)S(1)} all-to-all(bf16[32,8,1024]{2,0,1:T(8,128)(2,1)S(1)} %bitcast.106), channel_id=1, replica_groups=mesh['dp'=32,'tensor'=8] {'tensor'}, dimensions={1} | all-to-all | bytes 1048576 | tf_op jit(solution)/shard_map/all_to_all | solution.py:12
  189.8 1.0 fusion.20
  190.9 62.3 %all-reduce.6.cloned.1.call-done = f32[256,256]{1,0:T(8,128)} async-done(((f32[256,256]{1,0:T(8,128)}), f32[256,256]{1,0:T(8,128)}) %all-reduce.6.cloned.1.call-update) | async-done | bytes 262160 | tf_op jit(solution)/shard_map/psum | solution.py:91
  253.1 0.8 bitcast_dynamic-update-slice_fusion.3
  253.9 43.9 %all_gather.20 = bf16[32,8192]{1,0:T(8,128)(2,1)S(1)} all-gather(bf16[32,256]{1,0:T(8,128)(2,1)S(1)} %get-tuple-element.17), channel_id=1, replica_groups=mesh['dp'=32,'tensor'=8] {'dp'}, dimensions={1}, use_global_device_ids=true | all-gather | bytes 540672 | tf_op jit(solution)/shard_map/all_gather | solution.py:11
  297.8 12.8 %all_to_all.96 = bf16[32,8,1024]{2,0,1:T(8,128)(2,1)S(1)} all-to-all(bf16[32,8,1024]{2,0,1:T(8,128)(2,1)S(1)} %bitcast.109), channel_id=1, replica_groups=mesh['dp'=32,'tensor'=8] {'tensor'}, dimensions={1} | all-to-all | bytes 1048576 | tf_op jit(solution)/shard_map/all_to_all | solution.py:12
  310.7 1.0 fusion.21
  311.7 62.2 %all-reduce.8.cloned.1.call-done = f32[256,256]{1,0:T(8,128)} async-done(((f32[256,256]{1,0:T(8,128)}), f32[256,256]{1,0:T(8,128)}) %all-reduce.8.cloned.1.call-update) | async-done | bytes 262160 | tf_op jit(solution)/shard_map/psum | solution.py:91
  373.9 0.8 bitcast_dynamic-update-slice_fusion.2
  374.7 43.9 %all_gather.21 = bf16[32,8192]{1,0:T(8,128)(2,1)S(1)} all-gather(bf16[32,256]{1,0:T(8,128)(2,1)S(1)} %get-tuple-element.15), channel_id=1, replica_groups=mesh['dp'=32,'tensor'=8] {'dp'}, dimensions={1}, use_global_device_ids=true | all-gather | bytes 540672 | tf_op jit(solution)/shard_map/all_gather | solution.py:11
  418.6 12.8 %all_to_all.97 = bf16[32,8,1024]{2,0,1:T(8,128)(2,1)S(1)} all-to-all(bf16[32,8,1024]{2,0,1:T(8,128)(2,1)S(1)} %bitcast.112), channel_id=1, replica_groups=mesh['dp'=32,'tensor'=8] {'tensor'}, dimensions={1} | all-to-all | bytes 1048576 | tf_op jit(solution)/shard_map/all_to_all | solution.py:12
  431.5 1.0 fusion.22
  432.5 62.2 %all-reduce.10.cloned.1.call-done = f32[256,256]{1,0:T(8,128)} async-done(((f32[256,256]{1,0:T(8,128)}), f32[256,256]{1,0:T(8,128)}) %all-reduce.10.cloned.1.call-update) | async-done | bytes 262160 | tf_op jit(solution)/shard_map/psum | solution.py:91
  494.7 0.8 bitcast_dynamic-update-slice_fusion.1
  495.5 43.9 %all_gather.22 = bf16[32,8192]{1,0:T(8,128)(2,1)S(1)} all-gather(bf16[32,256]{1,0:T(8,128)(2,1)S(1)} %get-tuple-element.13), channel_id=1, replica_groups=mesh['dp'=32,'tensor'=8] {'dp'}, dimensions={1}, use_global_device_ids=true | all-gather | bytes 540672 | tf_op jit(solution)/shard_map/all_gather | solution.py:11
  539.5 12.8 %all_to_all.98 = bf16[32,8,1024]{2,0,1:T(8,128)(2,1)S(1)} all-to-all(bf16[32,8,1024]{2,0,1:T(8,128)(2,1)S(1)} %bitcast.115), channel_id=1, replica_groups=mesh['dp'=32,'tensor'=8] {'tensor'}, dimensions={1} | all-to-all | bytes 1048576 | tf_op jit(solution)/shard_map/all_to_all | solution.py:12
  552.3 1.0 fusion.23
  553.3 62.2 %all-reduce.12.cloned.1.call-done = f32[256,256]{1,0:T(8,128)} async-done(((f32[256,256]{1,0:T(8,128)}), f32[256,256]{1,0:T(8,128)}) %all-reduce.12.cloned.1.call-update) | async-done | bytes 262160 | tf_op jit(solution)/shard_map/psum | solution.py:91
  615.5 0.8 bitcast_dynamic-update-slice_fusion
  616.3 43.9 %all_gather.23 = bf16[32,8192]{1,0:T(8,128)(2,1)S(1)} all-gather(bf16[32,256]{1,0:T(8,128)(2,1)S(1)} %get-tuple-element.11), channel_id=1, replica_groups=mesh['dp'=32,'tensor'=8] {'dp'}, dimensions={1}, use_global_device_ids=true | all-gather | bytes 540672 | tf_op jit(solution)/shard_map/all_gather | solution.py:11
  660.3 12.8 %all_to_all.99 = bf16[32,8,1024]{2,0,1:T(8,128)(2,1)S(1)} all-to-all(bf16[32,8,1024]{2,0,1:T(8,128)(2,1)S(1)} %bitcast.118), channel_id=1, replica_groups=mesh['dp'=32,'tensor'=8] {'tensor'}, dimensions={1} | all-to-all | bytes 1048576 | tf_op jit(solution)/shard_map/all_to_all | solution.py:12
  673.1 1.0 fusion.24
  674.8 61.6 %all-reduce.14.cloned.1.call-done = f32[256,256]{1,0:T(8,128)} async-done(((f32[256,256]{1,0:T(8,128)}), f32[256,256]{1,0:T(8,128)}) %all-reduce.14.cloned.1.call-update) | async-done | bytes 262160 | tf_op jit(solution)/shard_map/psum | solution.py:91
  (45 shorter events, 4.4 us)
Async XLA Ops:
  7.2 87.5 %copy-start = (bf16[1024,256]{1,0:T(8,128)(2,1)S(1)}, bf16[1024,256]{1,0:T(8,128)(2,1)}, u32[]{:S(2)}) copy-start(bf16[1024,256]{1,0:T(8,128)(2,1)} %param.18) | copy-start | bytes 1572868
  7.2 4.8 copy-start.2
  7.2 87.5 %all-gather.2.cloned.1.call-start = ((), (), s32[]{:S(2)}) async-start(), calls=%async_computation.6 | async-start | bytes 3244032 | tf_op jit(solution)/shard_map/all_gather | solution.py:68
  12.9 85.8 %copy-start.3 = (bf16[32,6,256]{2,0,1:T(8,128)(2,1)S(1)}, bf16[32,6,256]{2,0,1:T(8,128)(2,1)}, u32[]{:S(2)}) copy-start(bf16[32,6,256]{2,0,1:T(8,128)(2,1)} %param.17) | copy-start | bytes 294916
  12.9 86.0 %copy-start.5 = (s32[32]{0:T(128)S(1)}, s32[32]{0:T(128)}, u32[]{:S(2)}) copy-start(s32[32]{0:T(128)} %param.16) | copy-start | bytes 388
  12.9 118.9 %reduce-scatter.2.cloned.1.call-start = ((), (), s32[]{:S(2)}) async-start(), calls=%async_computation.7 | async-start | bytes 1769472 | tf_op jit(solution)/shard_map/reduce_scatter | solution.py:72
  98.7 91.1 %copy-start.1 = (bf16[1024,256]{1,0:T(8,128)(2,1)S(1)}, bf16[1024,256]{1,0:T(8,128)(2,1)}, u32[]{:S(2)}) copy-start(bf16[1024,256]{1,0:T(8,128)(2,1)} %param.19) | copy-start | bytes 1572868
  98.7 154.4 %all-reduce.6.cloned.1.call-start = ((), (), s32[]{:S(2)}) async-start(), calls=%async_computation.8 | async-start | bytes 524288 | tf_op jit(solution)/shard_map/psum | solution.py:91
  190.8 183.1 %all-reduce.8.cloned.1.call-start = ((), (), s32[]{:S(2)}) async-start(), calls=%async_computation.9 | async-start | bytes 524288 | tf_op jit(solution)/shard_map/psum | solution.py:91
  311.7 183.1 %all-reduce.10.cloned.1.call-start = ((), (), s32[]{:S(2)}) async-start(), calls=%async_computation.10 | async-start | bytes 524288 | tf_op jit(solution)/shard_map/psum | solution.py:91
  432.5 183.1 %all-reduce.12.cloned.1.call-start = ((), (), s32[]{:S(2)}) async-start(), calls=%async_computation.11 | async-start | bytes 524288 | tf_op jit(solution)/shard_map/psum | solution.py:91
  553.3 183.1 %all-reduce.14.cloned.1.call-start = ((), (), s32[]{:S(2)}) async-start(), calls=%async_computation.12 | async-start | bytes 524288 | tf_op jit(solution)/shard_map/psum | solution.py:91
  737.1 0.6 copy-start.4
Sparse Core Ops, SparseCore 0:
  13.0 81.5 all-gather.1
  98.8 32.9 reduce-scatter.1
  190.9 62.1 all-reduce.5
  311.8 62.0 all-reduce.7
  432.6 62.1 all-reduce.9
  553.4 62.0 all-reduce.11
  674.2 62.1 all-reduce.13
where the time goes:
time: 745 us
  waiting for transfers between devices  425 us (57%)
  blocking collectives  284 us (38%)
  between operations  14.3 us (2%)
  matrix products  12.6 us (2%)
    psum x5, waiting for transfers between devices, per_device(): lax.psum(jnp.dot(current, draft_weight, preferred_element_type=jnp.float3...  311 us
    all_gather x5, blocking collectives, widen(): wide_rows = lax.all_gather(drafted_rows, 'dp', axis=1, tiled=True)  220 us
    all_gather x1, waiting for transfers between devices, per_device(): lax.all_gather(attended, 'dp', axis=0, tiled=True)  81.7 us
    all_to_all x5, blocking collectives, widen(): lax.all_to_all(wide_rows, 'tensor', split_axis=1, concat_axis=0, tiled=True)  64 us
    reduce_scatter x1, waiting for transfers between devices, per_device(): lax.psum_scatter(partial_out, 'tensor', scatter_dimension=0, tiled=True)  32.9 us
  transfers between devices with their start and end apart: 7, of which 7 were waited for; matrix products, arithmetic and copies ran while one was open for 0% of the time, Pallas kernels for 0%

commit v1 on v0

--- a/solution.py
+++ b/solution.py
@@ -8,7 +8,10 @@
 
 
 def widen(drafted_rows):
-    wide_rows = lax.all_gather(drafted_rows, "dp", axis=1, tiled=True)
+    peers = lax.axis_size("dp")
+    blocks = jnp.stack([drafted_rows for _ in range(peers)])
+    blocks = lax.all_to_all(blocks, "dp", split_axis=0, concat_axis=0)
+    wide_rows = jnp.concatenate(blocks, axis=1)
     return lax.all_to_all(wide_rows, "tensor", split_axis=1, concat_axis=0, tiled=True)
 
 

time: 745 us -> 653 us (0.88)
  blocking collectives: 284 us -> 190 us
    all_gather x5 -> x0, blocking collectives: 220 us -> none  [widen(): wide_rows = lax.all_gather(drafted_rows, 'dp', axis=1, tiled=True)]
    all_to_all x0 -> x5, blocking collectives: none -> 117 us  [widen(): blocks = lax.all_to_all(blocks, 'dp', split_axis=0, concat_axis=0)]
    all_to_all x5, blocking collectives: 64 us -> 73.7 us  [widen(): lax.all_to_all(wide_rows, 'tensor', split_axis=1, concat_axis=0, tiled=True)]
where the time goes in v1:
time: 653 us; the launch traced here: 652 us
  waiting for transfers between devices  421 us (64%)
  blocking collectives  190 us (29%)
  between operations  14.4 us (2%)
  matrix products  12.6 us (2%)
  local copies, waits for them, and re-layouts  6.88 us (1%)
    psum x5, waiting for transfers between devices, per_device(): lax.psum(jnp.dot(current, draft_weight, preferred_element_type=jnp.float3...  306 us
    all_to_all x5, blocking collectives, widen(): blocks = lax.all_to_all(blocks, 'dp', split_axis=0, concat_axis=0)  117 us
    all_gather x1, waiting for transfers between devices, per_device(): lax.all_gather(attended, 'dp', axis=0, tiled=True)  81.7 us
    all_to_all x5, blocking collectives, widen(): lax.all_to_all(wide_rows, 'tensor', split_axis=1, concat_axis=0, tiled=True)  73.7 us
    reduce_scatter x1, waiting for transfers between devices, per_device(): lax.psum_scatter(partial_out, 'tensor', scatter_dimension=0, tiled=True)  32.9 us
  transfers between devices with their start and end apart: 7, of which 7 were waited for; matrix products, arithmetic and copies ran while one was open for 0% of the time, Pallas kernels for 0%

profile of v1, /device:TPU:8, one launch (start us, length us, event | category | flops | bytes accessed | tf_op | source)
XLA Modules:
  0.0 651.8 jit_solution(4109693385243947342)
XLA Ops:
  7.2 0.8 iota_compare_fusion.1
  8.1 1.4 fusion.17
  9.5 1.2 fusion.18
  11.1 0.9 fusion.10
  13.0 81.7 %all-gather.2.cloned.1.call-done = bf16[1536,1024]{1,0:T(8,128)(2,1)} async-done(((bf16[48,1024]{1,0:T(8,128)(2,1)}), bf16[1536,1024]{1,0:T(8,128)(2,1)}) %all-gather.2.cloned.1.call-update) | async-done | bytes 3145744 | tf_op jit(solution)/shard_map/all_gather | solution.py:71
  94.7 4.0 fusion.19
  99.0 32.9 %reduce-scatter.2.cloned.1.call-done = f32[192,256]{1,0:T(8,128)} async-done(((f32[1536,256]{1,0:T(8,128)}), f32[192,256]{1,0:T(8,128)}) %reduce-scatter.2.cloned.1.call-update) | async-done | bytes 196624 | tf_op jit(solution)/shard_map/reduce_scatter | solution.py:75
  131.9 0.9 add_convert_fusion
  133.1 22.9 %all_to_all.120 = bf16[32,32,256]{2,1,0:T(8,128)(2,1)S(1)} all-to-all(bf16[32,32,256]{2,1,0:T(8,128)(2,1)S(1)} %stack.22), channel_id=1, replica_groups=mesh['dp'=32,'tensor'=8] {'dp'}, dimensions={0} | all-to-all | bytes 1048576 | tf_op jit(solution)/shard_map/all_to_all | solution.py:13
  156.9 13.9 %all_to_all.121 = bf16[32,8,1024]{2,0,1:T(8,128)(2,1)S(1)} all-to-all(bf16[32,8,1024]{2,0,1:T(8,128)(2,1)S(1)} %copy.38), channel_id=1, replica_groups=mesh['dp'=32,'tensor'=8] {'tensor'}, dimensions={1} | all-to-all | bytes 1048576 | tf_op jit(solution)/shard_map/all_to_all | solution.py:15
  170.9 1.0 fusion.20
  171.9 62.2 %all-reduce.6.cloned.1.call-done = f32[256,256]{1,0:T(8,128)} async-done(((f32[256,256]{1,0:T(8,128)}), f32[256,256]{1,0:T(8,128)}) %all-reduce.6.cloned.1.call-update) | async-done | bytes 262160 | tf_op jit(solution)/shard_map/psum | solution.py:94
  234.1 0.8 bitcast_dynamic-update-slice_fusion.3
  234.9 23.4 %all_to_all.122 = bf16[32,32,256]{2,1,0:T(8,128)(2,1)S(1)} all-to-all(bf16[32,32,256]{2,1,0:T(8,128)(2,1)S(1)} %stack.24), channel_id=1, replica_groups=mesh['dp'=32,'tensor'=8] {'dp'}, dimensions={0} | all-to-all | bytes 1048576 | tf_op jit(solution)/shard_map/all_to_all | solution.py:13
  259.3 14.9 %all_to_all.123 = bf16[32,8,1024]{2,0,1:T(8,128)(2,1)S(1)} all-to-all(bf16[32,8,1024]{2,0,1:T(8,128)(2,1)S(1)} %copy.40), channel_id=1, replica_groups=mesh['dp'=32,'tensor'=8] {'tensor'}, dimensions={1} | all-to-all | bytes 1048576 | tf_op jit(solution)/shard_map/all_to_all | solution.py:15
  274.2 1.0 fusion.21
  275.3 61.2 %all-reduce.8.cloned.1.call-done = f32[256,256]{1,0:T(8,128)} async-done(((f32[256,256]{1,0:T(8,128)}), f32[256,256]{1,0:T(8,128)}) %all-reduce.8.cloned.1.call-update) | async-done | bytes 262160 | tf_op jit(solution)/shard_map/psum | solution.py:94
  336.5 0.8 bitcast_dynamic-update-slice_fusion.2
  337.3 23.4 %all_to_all.124 = bf16[32,32,256]{2,1,0:T(8,128)(2,1)S(1)} all-to-all(bf16[32,32,256]{2,1,0:T(8,128)(2,1)S(1)} %stack.26), channel_id=1, replica_groups=mesh['dp'=32,'tensor'=8] {'dp'}, dimensions={0} | all-to-all | bytes 1048576 | tf_op jit(solution)/shard_map/all_to_all | solution.py:13
  361.7 14.9 %all_to_all.125 = bf16[32,8,1024]{2,0,1:T(8,128)(2,1)S(1)} all-to-all(bf16[32,8,1024]{2,0,1:T(8,128)(2,1)S(1)} %copy.42), channel_id=1, replica_groups=mesh['dp'=32,'tensor'=8] {'tensor'}, dimensions={1} | all-to-all | bytes 1048576 | tf_op jit(solution)/shard_map/all_to_all | solution.py:15
  376.6 1.0 fusion.22
  377.7 61.2 %all-reduce.10.cloned.1.call-done = f32[256,256]{1,0:T(8,128)} async-done(((f32[256,256]{1,0:T(8,128)}), f32[256,256]{1,0:T(8,128)}) %all-reduce.10.cloned.1.call-update) | async-done | bytes 262160 | tf_op jit(solution)/shard_map/psum | solution.py:94
  438.8 0.8 bitcast_dynamic-update-slice_fusion.1
  439.6 23.4 %all_to_all.126 = bf16[32,32,256]{2,1,0:T(8,128)(2,1)S(1)} all-to-all(bf16[32,32,256]{2,1,0:T(8,128)(2,1)S(1)} %stack.28), channel_id=1, replica_groups=mesh['dp'=32,'tensor'=8] {'dp'}, dimensions={0} | all-to-all | bytes 1048576 | tf_op jit(solution)/shard_map/all_to_all | solution.py:13
  464.0 14.9 %all_to_all.127 = bf16[32,8,1024]{2,0,1:T(8,128)(2,1)S(1)} all-to-all(bf16[32,8,1024]{2,0,1:T(8,128)(2,1)S(1)} %copy.44), channel_id=1, replica_groups=mesh['dp'=32,'tensor'=8] {'tensor'}, dimensions={1} | all-to-all | bytes 1048576 | tf_op jit(solution)/shard_map/all_to_all | solution.py:15
  478.9 1.0 fusion.23
  480.0 61.2 %all-reduce.12.cloned.1.call-done = f32[256,256]{1,0:T(8,128)} async-done(((f32[256,256]{1,0:T(8,128)}), f32[256,256]{1,0:T(8,128)}) %all-reduce.12.cloned.1.call-update) | async-done | bytes 262160 | tf_op jit(solution)/shard_map/psum | solution.py:94
  541.2 0.8 bitcast_dynamic-update-slice_fusion
  542.0 23.4 %all_to_all.128 = bf16[32,32,256]{2,1,0:T(8,128)(2,1)S(1)} all-to-all(bf16[32,32,256]{2,1,0:T(8,128)(2,1)S(1)} %stack.30), channel_id=1, replica_groups=mesh['dp'=32,'tensor'=8] {'dp'}, dimensions={0} | all-to-all | bytes 1048576 | tf_op jit(solution)/shard_map/all_to_all | solution.py:13
  566.4 14.9 %all_to_all.129 = bf16[32,8,1024]{2,0,1:T(8,128)(2,1)S(1)} all-to-all(bf16[32,8,1024]{2,0,1:T(8,128)(2,1)S(1)} %copy.46), channel_id=1, replica_groups=mesh['dp'=32,'tensor'=8] {'tensor'}, dimensions={1} | all-to-all | bytes 1048576 | tf_op jit(solution)/shard_map/all_to_all | solution.py:15
  581.3 1.0 fusion.24
  583.0 60.5 %all-reduce.14.cloned.1.call-done = f32[256,256]{1,0:T(8,128)} async-done(((f32[256,256]{1,0:T(8,128)}), f32[256,256]{1,0:T(8,128)}) %all-reduce.14.cloned.1.call-update) | async-done | bytes 262160 | tf_op jit(solution)/shard_map/psum | solution.py:94
  (60 shorter events, 9.0 us)
Async XLA Ops:
  7.2 87.5 %copy-start = (bf16[1024,256]{1,0:T(8,128)(2,1)S(1)}, bf16[1024,256]{1,0:T(8,128)(2,1)}, u32[]{:S(2)}) copy-start(bf16[1024,256]{1,0:T(8,128)(2,1)} %param.18) | copy-start | bytes 1572868
  7.2 4.8 copy-start.2
  7.2 87.5 %all-gather.2.cloned.1.call-start = ((), (), s32[]{:S(2)}) async-start(), calls=%async_computation.11 | async-start | bytes 3244032 | tf_op jit(solution)/shard_map/all_gather | solution.py:71
  12.9 85.8 %copy-start.3 = (bf16[32,6,256]{2,0,1:T(8,128)(2,1)S(1)}, bf16[32,6,256]{2,0,1:T(8,128)(2,1)}, u32[]{:S(2)}) copy-start(bf16[32,6,256]{2,0,1:T(8,128)(2,1)} %param.17) | copy-start | bytes 294916
  12.9 85.9 %copy-start.5 = (s32[32]{0:T(128)S(1)}, s32[32]{0:T(128)}, u32[]{:S(2)}) copy-start(s32[32]{0:T(128)} %param.16) | copy-start | bytes 388
  12.9 119.0 %reduce-scatter.2.cloned.1.call-start = ((), (), s32[]{:S(2)}) async-start(), calls=%async_computation.12 | async-start | bytes 1769472 | tf_op jit(solution)/shard_map/reduce_scatter | solution.py:75
  98.7 135.4 %all-reduce.6.cloned.1.call-start = ((), (), s32[]{:S(2)}) async-start(), calls=%async_computation.13 | async-start | bytes 524288 | tf_op jit(solution)/shard_map/psum | solution.py:94
  132.8 38.0 %copy-start.1 = (bf16[1024,256]{1,0:T(8,128)(2,1)S(1)}, bf16[1024,256]{1,0:T(8,128)(2,1)}, u32[]{:S(2)}) copy-start(bf16[1024,256]{1,0:T(8,128)(2,1)} %param.19) | copy-start | bytes 1572868
  171.9 164.6 %all-reduce.8.cloned.1.call-start = ((), (), s32[]{:S(2)}) async-start(), calls=%async_computation.14 | async-start | bytes 524288 | tf_op jit(solution)/shard_map/psum | solution.py:94
  275.3 163.6 %all-reduce.10.cloned.1.call-start = ((), (), s32[]{:S(2)}) async-start(), calls=%async_computation.15 | async-start | bytes 524288 | tf_op jit(solution)/shard_map/psum | solution.py:94
  377.6 163.6 %all-reduce.12.cloned.1.call-start = ((), (), s32[]{:S(2)}) async-start(), calls=%async_computation.16 | async-start | bytes 524288 | tf_op jit(solution)/shard_map/psum | solution.py:94
  480.0 163.6 %all-reduce.14.cloned.1.call-start = ((), (), s32[]{:S(2)}) async-start(), calls=%async_computation.17 | async-start | bytes 524288 | tf_op jit(solution)/shard_map/psum | solution.py:94
  644.3 0.6 copy-start.4
Sparse Core Ops, SparseCore 0:
  13.0 81.5 all-gather.1
  98.8 33.0 reduce-scatter.1
  172.0 62.0 all-reduce.5
  275.4 61.0 all-reduce.7
  377.7 61.0 all-reduce.9
  480.1 61.0 all-reduce.11
  582.4 61.0 all-reduce.13
